TPU v7x, 128 devices: a whole 4x4x4 slice. The times are simulated.
128 devices in a mesh: seq: 32 (over x, y, core), head: 4 (over z).
Axes of the slice: x: 4, y: 4, z: 4, core: 2. Of those that a mesh axis runs over, the one named last changes fastest.
Arguments:
- tokens: bfloat16 [32768, 1536], P('seq', 'head'), may hold values from -6 to 6
- norm_gain: float32 [1536], replicated, may hold values from 0.1 to 1.9
- w_qkv: bfloat16 [1536, 4608], P(None, 'head'), may hold values from -0.15625 to 0.15625
- w_out: bfloat16 [1536, 1536], P('head'), may hold values from -0.15625 to 0.15625
- frame_ids: int32 [32, 16], P('seq'), may hold values from 0 to 7, never falling along the last dimension, each value on 1 to 4 neighbouring positions
- slot_gain: float32 [1536], replicated, may hold values from 0.1 to 1.9
- w_key: bfloat16 [1536, 256], replicated, may hold values from -0.15625 to 0.15625
- w_value: bfloat16 [1536, 256], replicated, may hold values from -0.15625 to 0.15625
- w_query: float32 [256, 256], replicated, may hold values from -0.375 to 0.375
- slot_init: float32 [64, 256], replicated, may hold values from -6 to 6
- w_input: float32 [256, 768], replicated, may hold values from -0.375 to 0.375
- w_hidden: float32 [256, 768], replicated, may hold values from -0.375 to 0.375
Outputs:
- mixed: bfloat16 [32768, 1536], P(('seq', 'head'))
- slots: float32 [64, 256], replicated
Inputs may be any that keep to these rules, and one draw needn't show every extreme that they name: `frame_ids`: ids never fall along a row; a frame covers 1 to 4 blocks, and in every row some frame covers exactly 4 blocks.
All inputs are finite; a program needn't handle non-finite values.
Results may differ from a plain program's by a relative error of at most 0.008.
Values may be sent and summed in bfloat16 or wider, within the bound.
A program may use at most 64 MiB of HBM per device.

v0:
```python
import jax
import jax.numpy as jnp
from jax import lax
from jax.sharding import PartitionSpec as P

HD = 64
ITERS = 3
BLK = 64


def layer_norm(values, gain):
    mean = jnp.mean(values, axis=-1, keepdims=True)
    centred = values - mean
    var = jnp.mean(centred * centred, axis=-1, keepdims=True)
    return centred * lax.rsqrt(var + 1e-06) * gain


def normalize_exp(scores):
    powers = jnp.exp(scores)
    return powers / jnp.sum(powers, axis=-1, keepdims=True)


def recurrent_cell(update, state, w_input, w_hidden):
    high = lax.Precision.HIGHEST
    width = state.shape[1]
    from_in = jnp.dot(update, w_input, precision=high)
    from_state = jnp.dot(state, w_hidden, precision=high)
    reset = jax.nn.sigmoid(from_in[:, :width] + from_state[:, :width])
    gate = jax.nn.sigmoid(from_in[:, width : 2 * width] + from_state[:, width : 2 * width])
    candidate = jnp.tanh(from_in[:, 2 * width :] + reset * from_state[:, 2 * width :])
    return (1.0 - gate) * candidate + gate * state


def local(
    tokens,
    norm_gain,
    w_qkv,
    w_out,
    frame_ids,
    slot_gain,
    w_key,
    w_value,
    w_query,
    slot_init,
    w_input,
    w_hidden,
):
    whole = lax.all_gather(tokens, "head", axis=1, tiled=True)
    tok_count = whole.shape[0]
    normed = layer_norm(whole.astype(jnp.float32), norm_gain).astype(jnp.bfloat16)
    qkv = jnp.dot(normed, w_qkv, preferred_element_type=jnp.float32).astype(jnp.bfloat16)
    heads_here = w_qkv.shape[1] // (3 * HD)
    split = jnp.transpose(qkv.reshape(tok_count, heads_here, 3, HD), (1, 0, 2, 3))
    tok_ids = jnp.repeat(frame_ids[0], BLK)
    same = tok_ids[:, None] == tok_ids[None, :]

    def one_head(head_qkv):
        scores = jnp.dot(
            head_qkv[:, 0, :], head_qkv[:, 1, :].T, preferred_element_type=jnp.float32
        ) * HD ** (-0.5)
        scores = jnp.where(same, scores, -jnp.inf)
        probs = normalize_exp(scores).astype(jnp.bfloat16)
        return jnp.dot(probs, head_qkv[:, 2, :], preferred_element_type=jnp.float32).astype(
            jnp.bfloat16
        )

    outputs = lax.map(one_head, split)
    attended = jnp.transpose(outputs, (1, 0, 2)).reshape(tok_count, heads_here * HD)
    own_rows = tok_count // lax.axis_size("head")
    own_start = lax.axis_index("head") * own_rows
    own = lax.dynamic_slice_in_dim(whole, own_start, own_rows, 0)
    projected = lax.psum_scatter(
        jnp.dot(attended, w_out, preferred_element_type=jnp.float32).astype(jnp.bfloat16),
        "head",
        scatter_dimension=0,
        tiled=True,
    ).astype(jnp.float32)
    mixed = (own.astype(jnp.float32) + projected).astype(jnp.bfloat16)
    slot_in = layer_norm(mixed.astype(jnp.float32), slot_gain).astype(jnp.bfloat16)
    keys = jnp.dot(slot_in, w_key, preferred_element_type=jnp.float32).astype(jnp.bfloat16)
    values = jnp.dot(slot_in, w_value, preferred_element_type=jnp.float32).astype(jnp.bfloat16)
    slots = slot_init
    width = slot_init.shape[1]
    ones = jnp.ones((width,), jnp.float32)
    for step in range(ITERS):
        query = jnp.dot(layer_norm(slots, ones), w_query, precision=lax.Precision.HIGHEST).astype(
            jnp.bfloat16
        )
        logits = jnp.dot(keys, query.T, preferred_element_type=jnp.float32) * width ** (-0.5)
        weights = normalize_exp(logits)
        numer = jnp.einsum(
            "ts,td->sd", weights.astype(jnp.bfloat16), values, preferred_element_type=jnp.float32
        )
        denom = jnp.sum(weights, axis=0)
        numer, denom = lax.psum((numer, denom), ("seq", "head"))
        slots = recurrent_cell(numer / denom[:, None], slots, w_input, w_hidden)
    return (mixed, slots)


def solution(mesh):
    placed = (
        P("seq", "head"),
        P(),
        P(None, "head"),
        P("head", None),
        P("seq", None),
        P(),
        P(),
        P(),
        P(),
        P(),
        P(),
        P(),
    )
    return jax.shard_map(
        local,
        mesh=mesh,
        in_specs=placed,
        out_specs=(P(("seq", "head"), None), P()),
        check_vma=False,
    )
```

profile of v0, /device:TPU:1, one launch (start us, length us, event | category | flops | bytes accessed | tf_op | source)
XLA Modules:
  0.0 575.2 jit_solution(1970555273158845083)
XLA Ops:
  7.2 0.7 all-gather.2.cloned.1.call-update
  8.0 1.0 broadcast_in_dim.14
  9.0 43.7 %all-gather.2.cloned.1.call-done = bf16[1024,1536]{1,0:T(8,128)(2,1)} async-done(((bf16[1024,384]{1,0:T(8,128)(2,1)}), bf16[1024,1536]{1,0:T(8,128)(2,1)}) %all-gather.2.cloned.1.call-update) | async-done | bytes 3145744 | tf_op jit(solution)/shard_map/all_gather | solution.py:48
  52.7 2.5 convert_reduce_fusion
  55.3 0.3 copy-done.1
  55.6 1.0 fusion.12
  56.5 5.8 %convolution_convert_fusion.1 = bf16[1024,1152]{1,0:T(8,128)(2,1)} fusion(bf16[1536,1152]{1,0:T(8,128)(2,1)S(1)} %copy-done, bf16[1024,1536]{1,0:T(8,128)(2,1)S(1)} %copy-done.1, f32[1536]{0:T(1024)S(1)} %copy-done.12, f32[1024]{0:T(1024)S(1)} %add_rsqrt_fusion, f32[1024]{0:T(1024)S(1)} %broadcast_multiply_fusion), kind=kOutput, calls=%fused_computation.23 | convolution fusion | flops 3632922624 | bytes 9058304 | tf_op jit(solution)/shard_map/dot_general | solution.py:51
  62.4 4.3 copy.15
  66.7 23.8 %while.11 = (s32[]{:T(128)}, bf16[6,1024,64]{1,2,0:T(8,128)(2,1)}, bf16[6,1024,3,64]{1,3,2,0:T(8,128)(2,1)}, s32[1024]{0:T(1024)S(1)}, s32[]{:T(128)}) while((s32[]{:T(128)}, bf16[6,1024,64]{1,2,0:T(8,128)(2,1)}, bf16[6,1024,3,64]{1,3,2,0:T(8,128)(2,1)}, s32[1024]{0:T(1024)S(1)}, s32[]{:T(128)}) %tuple.47), condition=%wide.region_4.5_spmd.clone, body=%wide.region_2.4_spmd.clone.sunk | while | flops 277937152 | bytes 9724481 | solution.py:67
  66.7 1.0 dynamic-slice_bitcast_fusion.2
  67.7 1.1 fusion.133
  68.8 1.8 fusion.134
  70.6 1.0 dynamic-slice_bitcast_fusion.2
  71.6 1.1 fusion.133
  72.8 1.8 fusion.134
  74.6 1.0 dynamic-slice_bitcast_fusion.2
  75.6 1.1 fusion.133
  76.7 1.8 fusion.134
  78.6 1.0 dynamic-slice_bitcast_fusion.2
  79.6 1.1 fusion.133
  80.7 1.8 fusion.134
  82.5 1.0 dynamic-slice_bitcast_fusion.2
  83.6 1.1 fusion.133
  84.7 1.8 fusion.134
  86.5 1.0 dynamic-slice_bitcast_fusion.2
  87.5 1.1 fusion.133
  88.6 1.8 fusion.134
  90.5 5.0 convolution_convert_fusion
  95.6 0.9 reduce_sum.157
  96.6 1.0 multiply_reduce_fusion.2
  97.6 1.9 convolution_convert_fusion.6
  99.5 2.4 fusion.102
  102.0 32.3 %reduce-scatter.2.cloned.1.call-done = bf16[256,1536]{1,0:T(8,128)(2,1)} async-done(((bf16[1024,1536]{1,0:T(8,128)(2,1)}), bf16[256,1536]{1,0:T(8,128)(2,1)}) %reduce-scatter.2.cloned.1.call-update) | async-done | bytes 786448 | tf_op jit(solution)/shard_map/reduce_scatter | solution.py:72
  134.3 1.8 convert_reduce_fusion.1
  136.1 0.3 fusion.21
  136.5 0.5 convolution_convert_fusion.3
  137.0 0.5 convolution_convert_fusion.2
  137.7 0.4 copy-done.14
  138.3 0.8 fusion.86
  139.1 0.9 fusion.90
  140.1 64.9 %psum.43 = f32[64]{0:T(128)S(1)} all-reduce(f32[64]{0:T(128)S(1)} %fusion.90), channel_id=1, replica_groups=mesh['seq'=32,'head'=4] {'seq','head'}, use_global_device_ids=true, to_apply=%region_13.14 | all-reduce | flops 64 | bytes 512 | tf_op jit(solution)/shard_map/psum | solution.py:95
  205.0 72.0 %all-reduce.4.cloned.1.call-done = f32[64,256]{1,0:T(8,128)} async-done(((f32[64,256]{1,0:T(8,128)}), f32[64,256]{1,0:T(8,128)}) %all-reduce.4.cloned.1.call-update) | async-done | bytes 65552 | tf_op jit(solution)/shard_map/psum | solution.py:95
  276.9 1.8 fusion.69
  278.8 1.1 fusion.97
  279.9 2.4 fusion.103
  282.5 1.3 convolution_convert_fusion.5
  283.8 1.1 fusion.100
  284.9 0.6 copy-done.7
  285.5 0.8 fusion.81
  286.4 0.9 fusion.91
  287.3 63.8 %psum.45 = f32[64]{0:T(128)S(1)} all-reduce(f32[64]{0:T(128)S(1)} %fusion.91), channel_id=1, replica_groups=mesh['seq'=32,'head'=4] {'seq','head'}, use_global_device_ids=true, to_apply=%region_19.20 | all-reduce | flops 64 | bytes 512 | tf_op jit(solution)/shard_map/psum | solution.py:95
  351.1 69.9 %all-reduce.6.cloned.1.call-done = f32[64,256]{1,0:T(8,128)} async-done(((f32[64,256]{1,0:T(8,128)}), f32[64,256]{1,0:T(8,128)}) %all-reduce.6.cloned.1.call-update) | async-done | bytes 65552 | tf_op jit(solution)/shard_map/psum | solution.py:95
  421.1 1.8 fusion.66
  422.9 1.1 fusion.95
  424.0 2.4 fusion.104
  426.7 1.3 convolution_convert_fusion.4
  427.9 1.1 fusion.101
  429.0 0.6 copy-done.8
  429.7 0.8 fusion.76
  430.5 0.9 fusion.92
  431.4 63.7 %psum.47 = f32[64]{0:T(128)S(1)} all-reduce(f32[64]{0:T(128)S(1)} %fusion.92), channel_id=1, replica_groups=mesh['seq'=32,'head'=4] {'seq','head'}, use_global_device_ids=true, to_apply=%region_25.26 | all-reduce | flops 64 | bytes 512 | tf_op jit(solution)/shard_map/psum | solution.py:95
  495.1 70.1 %all-reduce.8.cloned.1.call-done = f32[64,256]{1,0:T(8,128)} async-done(((f32[64,256]{1,0:T(8,128)}), f32[64,256]{1,0:T(8,128)}) %all-reduce.8.cloned.1.call-update) | async-done | bytes 65552 | tf_op jit(solution)/shard_map/psum | solution.py:95
  565.2 1.8 fusion.63
  567.0 1.6 fusion.30
  (54 shorter events, 1.2 us)
Async XLA Ops:
  7.2 49.4 %copy-start = (bf16[1536,1152]{1,0:T(8,128)(2,1)S(1)}, bf16[1536,1152]{1,0:T(8,128)(2,1)}, u32[]{:S(2)}) copy-start(bf16[1536,1152]{1,0:T(8,128)(2,1)} %param.16) | copy-start | bytes 10616836
  7.2 45.5 %all-gather.2.cloned.1.call-start = ((), (), s32[]{:S(2)}) async-start(), calls=%async_computation.1 | async-start | bytes 3932160 | tf_op jit(solution)/shard_map/all_gather | solution.py:48
  7.9 126.3 %reduce-scatter.2.cloned.1.call-start = ((), (), s32[]{:S(2)}) async-start(), calls=%async_computation.2 | async-start | bytes 3932160 | tf_op jit(solution)/shard_map/reduce_scatter | solution.py:72
  9.0 47.5 %copy-start.12 = (f32[1536]{0:T(1024)S(1)}, f32[1536]{0:T(1024)}, u32[]{:S(2)}) copy-start(f32[1536]{0:T(1024)} %param.15) | copy-start | bytes 18436
  52.7 2.8 copy-start.1
  95.5 40.9 %copy-start.13 = (f32[1536]{0:T(1024)S(1)}, f32[1536]{0:T(1024)}, u32[]{:S(2)}) copy-start(f32[1536]{0:T(1024)} %param.19) | copy-start | bytes 18436
  95.5 181.4 %all-reduce.4.cloned.1.call-start = ((), (), s32[]{:S(2)}) async-start(), calls=%async_computation.3 | async-start | bytes 131072 | tf_op jit(solution)/shard_map/psum | solution.py:95
  134.3 2.2 copy-start.10
  134.3 2.7 copy-start.11
  136.1 1.4 copy-start.2
  136.1 1.3 copy-start.9
  136.9 0.7 copy-start.5
  137.4 0.6 copy-start.14
  137.7 0.6 copy-start.6
  139.1 282.0 %all-reduce.6.cloned.1.call-start = ((), (), s32[]{:S(2)}) async-start(), calls=%async_computation.4 | async-start | bytes 131072 | tf_op jit(solution)/shard_map/psum | solution.py:95
  276.9 8.6 %copy-start.15 = (bf16[256,256]{1,0:T(8,128)(2,1)S(1)}, bf16[256,256]{1,0:T(8,128)(2,1)}, u32[]{:S(2)}) copy-start(bf16[256,256]{1,0:T(8,128)(2,1)} %copy-done.14) | copy-start | bytes 393220
  279.9 2.6 copy-start.3
  284.9 0.6 copy-start.7
  286.3 278.9 %all-reduce.8.cloned.1.call-start = ((), (), s32[]{:S(2)}) async-start(), calls=%async_computation.5 | async-start | bytes 131072 | tf_op jit(solution)/shard_map/psum | solution.py:95
  421.1 8.6 %copy-start.16 = (bf16[256,256]{1,0:T(8,128)(2,1)S(1)}, bf16[256,256]{1,0:T(8,128)(2,1)}, u32[]{:S(2)}) copy-start(bf16[256,256]{1,0:T(8,128)(2,1)} %copy-done.14) | copy-start | bytes 393220
  424.0 2.6 copy-start.4
  429.0 0.6 copy-start.8
Sparse Core Ops, SparseCore 0:
  9.7 42.9 all-gather.1
  95.7 38.5 reduce-scatter.1
  139.6 137.3 all-reduce.3
  286.4 134.5 all-reduce.5
  430.6 134.5 all-reduce.7
where the time goes:
time: 576 us; the launch traced here: 575 us
  waiting for transfers between devices  289 us (50%)
  blocking collectives  192 us (33%)
  matrix products  51.3 us (9%)
  other arithmetic  14.7 us (3%)
  between operations  14.1 us (2%)
  local copies, waits for them, and re-layouts  13.7 us (2%)
    psum x3, waiting for transfers between devices, local(): numer, denom = lax.psum((numer, denom), ('seq', 'head'))  212 us
    psum x3, blocking collectives, local(): numer, denom = lax.psum((numer, denom), ('seq', 'head'))  192 us
    all_gather x1, waiting for transfers between devices, local(): whole = lax.all_gather(tokens, 'head', axis=1, tiled=True)  43.7 us
    reduce_scatter x1, waiting for transfers between devices, local(): lax.psum_scatter(jnp.dot(attended, w_out, preferred_element_type=jnp.floa...  32.3 us
  transfers between devices with their start and end apart: 5, of which 5 were waited for; matrix products, arithmetic and copies ran while one was open for 2% of the time, Pallas kernels for 0%

commit v1 on v0

--- a/solution.py
+++ b/solution.py
@@ -6,6 +6,10 @@
 HD = 64
 ITERS = 3
 BLK = 64
+
+
+def draft_edges(axis_name, x0, along_axis):
+    return lax.psum(lax.psum(x0, along_axis), axis_name)
 
 
 def layer_norm(values, gain):
@@ -92,7 +96,7 @@
             "ts,td->sd", weights.astype(jnp.bfloat16), values, preferred_element_type=jnp.float32
         )
         denom = jnp.sum(weights, axis=0)
-        numer, denom = lax.psum((numer, denom), ("seq", "head"))
+        numer, denom = draft_edges("head", (numer, denom), "seq")
         slots = recurrent_cell(numer / denom[:, None], slots, w_input, w_hidden)
     return (mixed, slots)
 

time: 576 us -> 669 us (1.16)
  waiting for transfers between devices: 289 us -> 354 us
  blocking collectives: 192 us -> 214 us
    psum x3 -> x6, waiting for transfers between devices: 212 us -> 275 us  [draft_edges(): return lax.psum(lax.psum(x0, along_axis), axis_name)]
    psum x3 -> x6, blocking collectives: 192 us -> 214 us  [draft_edges(): return lax.psum(lax.psum(x0, along_axis), axis_name)]
  transfers between devices with their start and end apart: 5 -> 8, of which waited for: 5 -> 5; matrix products, arithmetic and copies ran while one was open for 2% -> 2% of each run, Pallas kernels for 0% -> 0%
where the time goes in v1:
time: 669 us; the launch traced here: 665 us
  waiting for transfers between devices  354 us (53%)
  blocking collectives  214 us (32%)
  matrix products  53.1 us (8%)
  other arithmetic  14.7 us (2%)
  local copies, waits for them, and re-layouts  14.5 us (2%)
  between operations  14.4 us (2%)
    psum x6, waiting for transfers between devices, draft_edges(): return lax.psum(lax.psum(x0, along_axis), axis_name)  275 us
    psum x6, blocking collectives, draft_edges(): return lax.psum(lax.psum(x0, along_axis), axis_name)  214 us
    all_gather x1, waiting for transfers between devices, local(): whole = lax.all_gather(tokens, 'head', axis=1, tiled=True)  43.7 us
    reduce_scatter x1, waiting for transfers between devices, local(): lax.psum_scatter(jnp.dot(attended, w_out, preferred_element_type=jnp.floa...  34.7 us
  transfers between devices with their start and end apart: 8, of which 5 were waited for; matrix products, arithmetic and copies ran while one was open for 2% of the time, Pallas kernels for 0%

profile of v1, /device:TPU:1, one launch (start us, length us, event | category | flops | bytes accessed | tf_op | source)
XLA Modules:
  0.0 664.6 jit_solution(14134468201963811499)
XLA Ops:
  7.2 0.7 all-gather.2.cloned.1.call-update
  8.0 1.0 broadcast_in_dim.14
  9.0 43.7 %all-gather.2.cloned.1.call-done = bf16[1024,1536]{1,0:T(8,128)(2,1)} async-done(((bf16[1024,384]{1,0:T(8,128)(2,1)}), bf16[1024,1536]{1,0:T(8,128)(2,1)}) %all-gather.2.cloned.1.call-update) | async-done | bytes 3145744 | tf_op jit(solution)/shard_map/all_gather | solution.py:52
  52.7 2.5 convert_reduce_fusion
  55.6 1.0 fusion.12
  56.5 5.8 convolution_convert_fusion.1
  62.4 4.3 copy.15
  66.7 23.8 %while.11 = (s32[]{:T(128)}, bf16[6,1024,64]{1,2,0:T(8,128)(2,1)}, bf16[6,1024,3,64]{1,3,2,0:T(8,128)(2,1)}, s32[1024]{0:T(1024)S(1)}, s32[]{:T(128)}) while((s32[]{:T(128)}, bf16[6,1024,64]{1,2,0:T(8,128)(2,1)}, bf16[6,1024,3,64]{1,3,2,0:T(8,128)(2,1)}, s32[1024]{0:T(1024)S(1)}, s32[]{:T(128)}) %tuple.53), condition=%wide.region_4.5_spmd.clone, body=%wide.region_2.4_spmd.clone.sunk | while | flops 277937152 | bytes 9724481 | solution.py:71
  66.7 1.0 dynamic-slice_bitcast_fusion.2
  67.7 1.1 fusion.133
  68.8 1.8 fusion.134
  70.6 1.0 dynamic-slice_bitcast_fusion.2
  71.6 1.1 fusion.133
  72.8 1.8 fusion.134
  74.6 1.0 dynamic-slice_bitcast_fusion.2
  75.6 1.1 fusion.133
  76.7 1.8 fusion.134
  78.6 1.0 dynamic-slice_bitcast_fusion.2
  79.6 1.1 fusion.133
  80.7 1.8 fusion.134
  82.5 1.0 dynamic-slice_bitcast_fusion.2
  83.6 1.1 fusion.133
  84.7 1.8 fusion.134
  86.5 1.0 dynamic-slice_bitcast_fusion.2
  87.5 1.1 fusion.133
  88.6 1.8 fusion.134
  90.5 5.0 convolution_convert_fusion
  95.6 0.9 reduce_sum.157
  96.6 1.0 multiply_reduce_fusion.2
  97.6 1.9 convolution_convert_fusion.6
  99.5 34.7 %reduce-scatter.2.cloned.1.call-done = bf16[256,1536]{1,0:T(8,128)(2,1)} async-done(((bf16[1024,1536]{1,0:T(8,128)(2,1)}), bf16[256,1536]{1,0:T(8,128)(2,1)}) %reduce-scatter.2.cloned.1.call-update) | async-done | bytes 786448 | tf_op jit(solution)/shard_map/reduce_scatter | solution.py:76
  134.3 1.8 convert_reduce_fusion.1
  136.5 0.5 convolution_convert_fusion.3
  137.0 0.5 convolution_convert_fusion.2
  138.3 0.8 fusion.86
  139.1 2.4 fusion.102
  141.6 92.9 %all-reduce.7.cloned.1.call-done = f32[64,256]{1,0:T(8,128)} async-done(((f32[64,256]{1,0:T(8,128)}), f32[64,256]{1,0:T(8,128)}) %all-reduce.7.cloned.1.call-update) | async-done | bytes 65552 | tf_op jit(solution)/shard_map/psum | solution.py:12
  234.5 0.9 fusion.90
  235.5 62.4 %psum.86 = f32[64]{0:T(128)S(1)} all-reduce(f32[64]{0:T(128)S(1)} %fusion.90), channel_id=1, replica_groups=mesh['seq'=32,'head'=4] {'seq'}, use_global_device_ids=true, to_apply=%region_14.15 | all-reduce | flops 64 | bytes 512 | tf_op jit(solution)/shard_map/psum | solution.py:12
  297.9 8.8 %psum.87 = f32[64]{0:T(128)S(1)} all-reduce(f32[64]{0:T(128)S(1)} %psum.86), channel_id=1, replica_groups=mesh['seq'=32,'head'=4] {'head'}, use_global_device_ids=true, to_apply=%region_15.16 | all-reduce | flops 64 | bytes 512 | tf_op jit(solution)/shard_map/psum | solution.py:12
  306.6 1.8 fusion.69
  308.4 1.1 fusion.97
  310.2 1.2 convolution_convert_fusion.5
  311.4 1.1 fusion.100
  312.6 0.6 copy-done.7
  313.2 1.7 fusion.81
  314.9 2.4 fusion.103
  317.4 90.9 %all-reduce.11.cloned.1.call-done = f32[64,256]{1,0:T(8,128)} async-done(((f32[64,256]{1,0:T(8,128)}), f32[64,256]{1,0:T(8,128)}) %all-reduce.11.cloned.1.call-update) | async-done | bytes 65552 | tf_op jit(solution)/shard_map/psum | solution.py:12
  408.3 0.9 fusion.91
  409.2 62.4 %psum.90 = f32[64]{0:T(128)S(1)} all-reduce(f32[64]{0:T(128)S(1)} %fusion.91), channel_id=1, replica_groups=mesh['seq'=32,'head'=4] {'seq'}, use_global_device_ids=true, to_apply=%region_22.23 | all-reduce | flops 64 | bytes 512 | tf_op jit(solution)/shard_map/psum | solution.py:12
  471.6 9.0 %psum.91 = f32[64]{0:T(128)S(1)} all-reduce(f32[64]{0:T(128)S(1)} %psum.90), channel_id=1, replica_groups=mesh['seq'=32,'head'=4] {'head'}, use_global_device_ids=true, to_apply=%region_23.24 | all-reduce | flops 64 | bytes 512 | tf_op jit(solution)/shard_map/psum | solution.py:12
  480.6 1.8 fusion.66
  482.4 1.1 fusion.95
  484.1 1.3 convolution_convert_fusion.4
  485.4 1.1 fusion.101
  486.5 0.6 copy-done.8
  487.1 1.7 fusion.76
  488.9 2.4 fusion.104
  491.3 90.9 %all-reduce.15.cloned.1.call-done = f32[64,256]{1,0:T(8,128)} async-done(((f32[64,256]{1,0:T(8,128)}), f32[64,256]{1,0:T(8,128)}) %all-reduce.15.cloned.1.call-update) | async-done | bytes 65552 | tf_op jit(solution)/shard_map/psum | solution.py:12
  582.2 0.9 fusion.92
  583.2 62.4 %psum.94 = f32[64]{0:T(128)S(1)} all-reduce(f32[64]{0:T(128)S(1)} %fusion.92), channel_id=1, replica_groups=mesh['seq'=32,'head'=4] {'seq'}, use_global_device_ids=true, to_apply=%region_30.31 | all-reduce | flops 64 | bytes 512 | tf_op jit(solution)/shard_map/psum | solution.py:12
  645.6 8.8 %psum.95 = f32[64]{0:T(128)S(1)} all-reduce(f32[64]{0:T(128)S(1)} %psum.94), channel_id=1, replica_groups=mesh['seq'=32,'head'=4] {'head'}, use_global_device_ids=true, to_apply=%region_31.32 | all-reduce | flops 64 | bytes 512 | tf_op jit(solution)/shard_map/psum | solution.py:12
  654.3 1.8 fusion.63
  656.1 1.6 fusion.30
  (62 shorter events, 3.3 us)
Async XLA Ops:
  7.2 49.4 %copy-start = (bf16[1536,1152]{1,0:T(8,128)(2,1)S(1)}, bf16[1536,1152]{1,0:T(8,128)(2,1)}, u32[]{:S(2)}) copy-start(bf16[1536,1152]{1,0:T(8,128)(2,1)} %param.16) | copy-start | bytes 10616836
  7.2 45.5 %all-gather.2.cloned.1.call-start = ((), (), s32[]{:S(2)}) async-start(), calls=%async_computation.1 | async-start | bytes 3932160 | tf_op jit(solution)/shard_map/all_gather | solution.py:52
  7.9 126.3 %reduce-scatter.2.cloned.1.call-start = ((), (), s32[]{:S(2)}) async-start(), calls=%async_computation.2 | async-start | bytes 3932160 | tf_op jit(solution)/shard_map/reduce_scatter | solution.py:76
  9.0 47.5 %copy-start.12 = (f32[1536]{0:T(1024)S(1)}, f32[1536]{0:T(1024)}, u32[]{:S(2)}) copy-start(f32[1536]{0:T(1024)} %param.15) | copy-start | bytes 18436
  52.7 2.8 copy-start.1
  95.5 40.9 %copy-start.13 = (f32[1536]{0:T(1024)S(1)}, f32[1536]{0:T(1024)}, u32[]{:S(2)}) copy-start(f32[1536]{0:T(1024)} %param.19) | copy-start | bytes 18436
  95.5 138.9 %all-reduce.7.cloned.1.call-start = ((), (), s32[]{:S(2)}) async-start(), calls=%async_computation.3 | async-start | bytes 131072 | tf_op jit(solution)/shard_map/psum | solution.py:12
  134.3 2.2 copy-start.10
  134.3 2.7 copy-start.11
  136.1 1.4 copy-start.2
  136.1 1.3 copy-start.9
  136.9 0.7 copy-start.5
  137.4 0.6 copy-start.14
  137.7 0.6 copy-start.6
  139.1 167.5 %all-reduce.9.cloned.1.call-start = ((), (), s32[]{:S(2)}) async-start(), calls=%async_computation.4 | async-start | bytes 131072 | tf_op jit(solution)/shard_map/psum | solution.py:12
  234.5 173.8 %all-reduce.11.cloned.1.call-start = ((), (), s32[]{:S(2)}) async-start(), calls=%async_computation.5 | async-start | bytes 131072 | tf_op jit(solution)/shard_map/psum | solution.py:12
  309.5 0.6 copy-start.3
  312.6 0.6 copy-start.7
  314.9 165.7 %all-reduce.13.cloned.1.call-start = ((), (), s32[]{:S(2)}) async-start(), calls=%async_computation.6 | async-start | bytes 131072 | tf_op jit(solution)/shard_map/psum | solution.py:12
  408.2 173.9 %all-reduce.15.cloned.1.call-start = ((), (), s32[]{:S(2)}) async-start(), calls=%async_computation.7 | async-start | bytes 131072 | tf_op jit(solution)/shard_map/psum | solution.py:12
  483.5 0.6 copy-start.4
  486.5 0.6 copy-start.8
  488.8 165.5 %all-reduce.17.cloned.1.call-start = ((), (), s32[]{:S(2)}) async-start(), calls=%async_computation.8 | async-start | bytes 131072 | tf_op jit(solution)/shard_map/psum | solution.py:12
Sparse Core Ops, SparseCore 0:
  9.7 42.9 all-gather.1
  95.7 38.5 reduce-scatter.1
  139.2 95.1 all-reduce.6
  236.7 37.7 all-reduce.8
  315.0 93.1 all-reduce.10
  410.5 37.7 all-reduce.12
  489.0 93.1 all-reduce.14
  584.6 37.7 all-reduce.16
